TPU v7x, 32 devices: a whole 2x2x4 slice. The times are simulated.
32 devices in a mesh: groups: 2 (over x), ctx: 16 (over z, y, core).
Axes of the slice: x: 2, y: 2, z: 4, core: 2. Of those that a mesh axis runs over, the one named last changes fastest.
Arguments:
- queries: bfloat16 [4096, 2048], P(('groups', 'ctx')), parts along dimension 0, may hold values from -6 to 6
- keys: bfloat16 [4096, 2048], P(('groups', 'ctx')), parts along dimension 0, may hold values from -6 to 6
- values: bfloat16 [4096, 2048], P(('groups', 'ctx')), parts along dimension 0, may hold values from -6 to 6
- out_grad: bfloat16 [4096, 2048], P(('groups', 'ctx')), parts along dimension 0, may hold values from -6 to 6
- conv_weight: float32 [8, 16], replicated, may hold values from -2 to 2
Outputs:
- dq: bfloat16 [4096, 2048], P(('groups', 'ctx')), parts along dimension 0
- dk: bfloat16 [4096, 2048], P(('groups', 'ctx')), parts along dimension 0
- dv: bfloat16 [4096, 2048], P(('groups', 'ctx')), parts along dimension 0
- dconv: float32 [16, 16], P('groups'), parts along dimension 0
There are 2 independent parts, one for each index of `groups`. A program takes and returns all parts, laid end to end along the dimension named above; an argument that names none is the same for every part. Nothing has to cross between parts.
All inputs are finite; a program needn't handle non-finite values.
Results may differ from a plain program's by a relative error of at most 0.024.
Values may be sent and summed in bfloat16 or wider, within the bound.
A program may use at most 128 MiB of HBM per device.

v0:
```python
import jax
import jax.numpy as jnp
from jax import lax
from jax.sharding import PartitionSpec as P


def compress(rows, conv_weight):
    count = rows.shape[0]
    stride, heads = conv_weight.shape
    shaped = rows.reshape(count // stride, stride, heads, -1).astype(jnp.float32)
    merged = jnp.einsum("cshd,sh->chd", shaped, conv_weight).astype(jnp.bfloat16)
    return merged.reshape(count // stride, -1)


def local(queries, keys, values, out_grad, conv_weight):
    count, width = queries.shape
    stride, heads = conv_weight.shape
    head_dim = width // heads
    rows_mem = count // stride
    scale = head_dim ** (-0.5)
    shard_id = lax.axis_index("ctx")
    total_mem = rows_mem * lax.axis_size("ctx")
    q3 = queries.reshape(count, heads, head_dim)
    k3 = keys.reshape(count, heads, head_dim)
    v3 = values.reshape(count, heads, head_dim)
    g3 = out_grad.reshape(count, heads, head_dim)
    mem_keys = compress(keys, conv_weight)
    mem_vals = compress(values, conv_weight)
    causal = jnp.arange(count)[:, None] >= jnp.arange(count)[None, :]
    local_scores = jnp.einsum("shd,thd->hst", q3, k3, preferred_element_type=jnp.float32) * scale
    local_scores = jnp.where(causal[None], local_scores, -1e30)
    high0 = local_scores.max(-1)
    local_prob = jnp.where(causal[None], jnp.exp(local_scores - high0[..., None]), 0.0)
    total0 = local_prob.sum(-1)
    accum0 = jnp.einsum("hst,thd->hsd", local_prob, v3.astype(jnp.float32))

    def score_block(block_keys):
        rows = block_keys.shape[0]
        keys_block = block_keys.reshape(rows, heads, head_dim)
        valid = jnp.arange(rows, dtype=jnp.int32) // rows_mem < shard_id
        scores = (
            jnp.einsum("shd,nhd->hsn", q3, keys_block, preferred_element_type=jnp.float32) * scale
        )
        return (valid, scores)

    all_keys, all_vals = (
        lax.all_gather(mem_keys, "ctx", axis=0, tiled=True),
        lax.all_gather(mem_vals, "ctx", axis=0, tiled=True),
    )
    high = high0
    total = total0
    accum = accum0
    rows = all_keys.shape[0]
    valid, scores = score_block(all_keys)
    scores = jnp.where(valid[None, None, :], scores, -1e30)
    new_high = jnp.maximum(high, scores.max(-1))
    prob = jnp.where(valid[None, None, :], jnp.exp(scores - new_high[..., None]), 0.0)
    factor = jnp.exp(high - new_high)
    vals_block = all_vals.reshape(rows, heads, head_dim)
    total = total * factor + prob.sum(-1)
    accum = accum * factor[..., None] + jnp.einsum(
        "hsn,nhd->hsd", prob, vals_block, preferred_element_type=jnp.float32
    )
    stats = (new_high, total, accum)
    high, total, accum = stats
    lse = high + jnp.log(total)
    output = accum / total[..., None]
    dsum = jnp.einsum("hsd,shd->hs", output, g3.astype(jnp.float32))
    valid_all, scores_all = score_block(all_keys)
    mem_prob = jnp.where(valid_all[None, None, :], jnp.exp(scores_all - lse[..., None]), 0.0)
    keys_all = all_keys.reshape(total_mem, heads, head_dim)
    vals_all = all_vals.reshape(total_mem, heads, head_dim)
    mem_dprob = jnp.einsum("shd,nhd->hsn", g3, vals_all, preferred_element_type=jnp.float32)
    mem_ds = (mem_prob * (mem_dprob - dsum[..., None])).astype(jnp.bfloat16)
    mem_pb = mem_prob.astype(jnp.bfloat16)
    dq_mem = jnp.einsum("hsn,nhd->shd", mem_ds, keys_all, preferred_element_type=jnp.float32)
    dk_part = jnp.einsum("hsn,shd->nhd", mem_ds, q3, preferred_element_type=jnp.float32) * scale
    dv_part = jnp.einsum("hsn,shd->nhd", mem_pb, g3, preferred_element_type=jnp.float32)
    summed = lax.psum_scatter(
        jnp.concatenate(
            (dk_part.reshape(total_mem, width), dv_part.reshape(total_mem, width)), axis=1
        ),
        "ctx",
        scatter_dimension=0,
        tiled=True,
    )
    dmem_k = summed[:, :width].reshape(rows_mem, heads, head_dim)
    dmem_v = summed[:, width:].reshape(rows_mem, heads, head_dim)
    local_p = jnp.where(causal[None], jnp.exp(local_scores - lse[..., None]), 0.0)
    local_dp = jnp.einsum("shd,thd->hst", g3, v3, preferred_element_type=jnp.float32)
    local_ds = (local_p * (local_dp - dsum[..., None])).astype(jnp.bfloat16)
    dq_all = (
        dq_mem + jnp.einsum("hst,thd->shd", local_ds, k3, preferred_element_type=jnp.float32)
    ) * scale
    dk_local = jnp.einsum("hst,shd->thd", local_ds, q3, preferred_element_type=jnp.float32) * scale
    dv_local = jnp.einsum(
        "hst,shd->thd", local_p.astype(jnp.bfloat16), g3, preferred_element_type=jnp.float32
    )
    spread_k = jnp.einsum("chd,sh->cshd", dmem_k, conv_weight).reshape(count, heads, head_dim)
    spread_v = jnp.einsum("chd,sh->cshd", dmem_v, conv_weight).reshape(count, heads, head_dim)
    dq = dq_all.reshape(count, width).astype(jnp.bfloat16)
    dk = (dk_local + spread_k).reshape(count, width).astype(jnp.bfloat16)
    dv = (dv_local + spread_v).reshape(count, width).astype(jnp.bfloat16)
    key_rows = keys.reshape(rows_mem, stride, heads, head_dim).astype(jnp.float32)
    val_rows = values.reshape(rows_mem, stride, heads, head_dim).astype(jnp.float32)
    partial_conv = jnp.einsum("chd,cshd->sh", dmem_k, key_rows) + jnp.einsum(
        "chd,cshd->sh", dmem_v, val_rows
    )
    dconv = lax.psum(partial_conv, "ctx")
    return (dq, dk, dv, dconv)


def solution(mesh):
    return jax.shard_map(
        local,
        mesh=mesh,
        in_specs=(
            P(("groups", "ctx"), None),
            P(("groups", "ctx"), None),
            P(("groups", "ctx"), None),
            P(("groups", "ctx"), None),
            P(),
        ),
        out_specs=(
            P(("groups", "ctx"), None),
            P(("groups", "ctx"), None),
            P(("groups", "ctx"), None),
            P("groups", None),
        ),
        check_vma=False,
    )
```

profile of v0, /device:TPU:0, one launch (start us, length us, event | category | flops | bytes accessed | tf_op | source)
XLA Modules:
  0.0 238.7 jit_solution(13422166051931242764)
XLA Ops:
  7.2 0.8 copy.90
  8.1 1.4 fusion.38
  10.2 1.3 fusion.36
  13.0 1.2 copy.80
  14.7 1.0 copy-done
  15.9 35.5 %all-gather.3.cloned.1.call-done = bf16[256,2048]{1,0:T(8,128)(2,1)} async-done(((bf16[16,2048]{1,0:T(8,128)(2,1)}), bf16[256,2048]{1,0:T(8,128)(2,1)}) %all-gather.3.cloned.1.call-update) | async-done | bytes 1048592 | tf_op jit(solution)/shard_map/all_gather | solution.py:47
  51.4 2.3 copy.58
  53.6 1.8 bitcast_reduce_fusion
  56.1 34.3 %all-gather.5.cloned.1.call-done = bf16[256,2048]{1,0:T(8,128)(2,1)} async-done(((bf16[16,2048]{1,0:T(8,128)(2,1)}), bf16[256,2048]{1,0:T(8,128)(2,1)}) %all-gather.5.cloned.1.call-update) | async-done | bytes 1048592 | tf_op jit(solution)/shard_map/all_gather | solution.py:48
  90.4 2.3 copy.63
  92.7 2.2 fusion.3
  94.9 0.8 fusion.13
  96.5 3.1 %fusion.19 = f32[16,256,128]{1,2,0:T(8,128)} fusion(bf16[128,16,128]{0,2,1:T(8,128)(2,1)} %copy.80, f32[16,256,128]{2,1,0:T(8,128)S(1)} %get-tuple-element.26, f32[16,128]{1,0:T(8,128)S(1)} %get-tuple-element.16, pred[256]{0:T(512)(128)(4,1)S(1)} %fusion.48), kind=kOutput, calls=%fused_computation.31 | convolution fusion | flops 136314880 | bytes 4727040 | tf_op jit(solution)/shard_map/hsn,shd->nhd/dot_general | solution.py:78
  99.6 0.9 multiply_convert_fusion
  100.5 1.0 copy-done.10
  101.9 1.8 copy.79
  103.7 4.5 %pad_maximum_fusion = f32[256,4096]{0,1:T(8,128)} fusion(f32[256,2048]{0,1:T(8,128)} %bitcast.140, f32[256,2048]{0,1:T(8,128)} %bitcast.141), kind=kLoop, calls=%fused_computation | loop fusion | flops 1048576 | bytes 8388608 | tf_op jit(solution)/shard_map/concatenate | solution.py:80
  108.2 5.6 %copy.125 = f32[256,4096]{1,0:T(8,128)} copy(f32[256,4096]{0,1:T(8,128)} %pad_maximum_fusion) | data formatting | bytes 8388608
  113.8 1.2 copy-done.2
  115.0 1.6 fusion.17
  117.2 0.8 copy-done.9
  118.3 1.0 copy.87
  119.3 66.5 %reduce-scatter.4.cloned.1.call-done = f32[16,4096]{1,0:T(8,128)} async-done(((f32[256,4096]{1,0:T(8,128)}), f32[16,4096]{1,0:T(8,128)}) %reduce-scatter.4.cloned.1.call-update) | async-done | bytes 262160
  185.8 1.0 fusion.56
  187.8 1.3 multiply_reduce_fusion
  191.6 30.1 %psum.7 = f32[8,16]{1,0:T(8,128)} all-reduce(f32[8,16]{1,0:T(8,128)S(1)} %add_bitcast_fusion), channel_id=1, replica_groups=mesh['groups'=2,'ctx'=16] {'ctx'}, use_global_device_ids=true, to_apply=%region_5.6 | all-reduce | flops 128 | bytes 1024 | tf_op jit(solution)/shard_map/psum | solution.py:109
  221.7 2.4 broadcast_multiply_fusion
  224.1 1.6 copy.86
  225.7 1.3 fusion.18
  227.0 2.1 copy.89
  229.1 1.6 copy.82
  231.2 1.0 copy.88
  (72 shorter events, 9.5 us)
Async XLA Ops:
  7.2 5.2 %copy-start.4 = (bf16[128,2048]{1,0:T(8,128)(2,1)S(1)}, bf16[128,2048]{1,0:T(8,128)(2,1)}, u32[]{:S(2)}) copy-start(bf16[128,2048]{1,0:T(8,128)(2,1)} %param.6) | copy-start | bytes 1572868
  7.2 5.5 %copy-start.16 = (bf16[128,2048]{1,0:T(8,128)(2,1)S(1)}, bf16[128,2048]{1,0:T(8,128)(2,1)}, u32[]{:S(2)}) copy-start(bf16[128,2048]{1,0:T(8,128)(2,1)} %param.5) | copy-start | bytes 1572868
  7.2 44.2 %all-gather.3.cloned.1.call-start = ((), (), s32[]{:S(2)}) async-start(), calls=%async_computation.1 | async-start | bytes 1114112 | tf_op jit(solution)/shard_map/all_gather | solution.py:47
  8.1 4.8 %copy-start.17 = (bf16[128,2048]{1,0:T(8,128)(2,1)S(1)}, bf16[128,2048]{1,0:T(8,128)(2,1)}, u32[]{:S(2)}) copy-start(bf16[128,2048]{1,0:T(8,128)(2,1)} %param.8) | copy-start | bytes 1572868
  10.2 80.2 %all-gather.5.cloned.1.call-start = ((), (), s32[]{:S(2)}) async-start(), calls=%async_computation.2 | async-start | bytes 1114112 | tf_op jit(solution)/shard_map/all_gather | solution.py:48
  12.3 173.5 %reduce-scatter.4.cloned.1.call-start = ((), (), s32[]{:S(2)}) async-start(), calls=%async_computation.3 | async-start | bytes 4456448
  12.6 2.1 copy-start.8
  14.7 1.0 copy-start
  92.7 2.2 copy-start.1
  92.7 2.2 copy-start.14
  94.9 19.0 %copy-start.18 = (f32[16,128]{1,0:T(8,128)}, f32[16,128]{1,0:T(8,128)S(1)}, u32[]{:S(2)}) copy-start(f32[16,128]{1,0:T(8,128)S(1)} %get-tuple-element.16) | copy-start | bytes 24580
  96.5 3.1 %copy-start.6 = (bf16[128,16,128]{0,2,1:T(8,128)(2,1)S(1)}, bf16[128,16,128]{0,2,1:T(8,128)(2,1)}, u32[]{:S(2)}) copy-start(bf16[128,16,128]{0,2,1:T(8,128)(2,1)} %copy.80) | copy-start | bytes 1572868
  96.5 3.1 %copy-start.15 = (bf16[256,2048]{0,1:T(8,128)(2,1)S(1)}, bf16[256,2048]{0,1:T(8,128)(2,1)}, u32[]{:S(2)}) copy-start(bf16[256,2048]{0,1:T(8,128)(2,1)} %copy.63) | copy-start | bytes 3145732
  100.5 1.0 copy-start.10
  113.8 1.2 copy-start.2
  115.0 1.6 copy-start.3
  115.0 1.7 copy-start.11
  116.7 1.5 copy-start.12
  116.7 1.2 copy-start.9
  187.7 2.9 %copy-start.5 = (bf16[128,2048]{1,0:T(8,128)(2,1)S(1)}, bf16[128,2048]{1,0:T(8,128)(2,1)}, u32[]{:S(2)}) copy-start(bf16[128,2048]{1,0:T(8,128)(2,1)} %param.6) | copy-start | bytes 1572868
  221.7 4.0 %copy-start.7 = (bf16[128,16,128]{0,2,1:T(8,128)(2,1)S(1)}, bf16[128,16,128]{0,2,1:T(8,128)(2,1)}, u32[]{:S(2)}) copy-start(bf16[128,16,128]{0,2,1:T(8,128)(2,1)} %copy.80) | copy-start | bytes 1572868
  221.7 4.0 %copy-start.19 = (f32[16,128]{1,0:T(8,128)S(1)}, f32[16,128]{1,0:T(8,128)}, u32[]{:S(2)}) copy-start(f32[16,128]{1,0:T(8,128)} %copy-done.18) | copy-start | bytes 24580
  227.0 3.7 %copy-start.13 = (bf16[16,128,128]{1,2,0:T(8,128)(2,1)S(1)}, bf16[16,128,128]{1,2,0:T(8,128)(2,1)}, u32[]{:S(2)}) copy-start(bf16[16,128,128]{1,2,0:T(8,128)(2,1)} %copy-done.12) | copy-start | bytes 1572868
Sparse Core Ops, SparseCore 0:
  10.7 40.5 all-gather.2
  53.5 36.8 all-gather.4
  114.0 71.7 reduce-scatter.3
where the time goes:
time: 239 us
  waiting for transfers between devices  136 us (57%)
  local copies, waits for them, and re-layouts  31.1 us (13%)
  blocking collectives  30.1 us (13%)
  matrix products  16.4 us (7%)
  between operations  14.1 us (6%)
  other arithmetic  10.6 us (4%)
    unnamed x4, waiting for transfers between devices  66.5 us
    all_gather x1, waiting for transfers between devices, local(): lax.all_gather(mem_keys, 'ctx', axis=0, tiled=True)  35.5 us
    all_gather x1, waiting for transfers between devices, local(): lax.all_gather(mem_vals, 'ctx', axis=0, tiled=True)  34.3 us
    psum x1, blocking collectives, local(): dconv = lax.psum(partial_conv, 'ctx')  30.1 us
    unnamed x52, local copies, waits for them, and re-layouts  17.3 us
  transfers between devices with their start and end apart: 3, of which 3 were waited for; matrix products, arithmetic and copies ran while one was open for 5% of the time, Pallas kernels for 0%

commit v1 on v0

--- a/solution.py
+++ b/solution.py
@@ -106,7 +106,11 @@
     partial_conv = jnp.einsum("chd,cshd->sh", dmem_k, key_rows) + jnp.einsum(
         "chd,cshd->sh", dmem_v, val_rows
     )
-    dconv = lax.psum(partial_conv, "ctx")
+    devices = lax.axis_size("ctx")
+    dconv, far = (partial_conv, 1)
+    while far < devices:
+        dconv = dconv + lax.ppermute(dconv, "ctx", [(i, i ^ far) for i in range(devices)])
+        far = 2 * far
     return (dq, dk, dv, dconv)
 
 

time: 239 us -> 218 us (0.912)
  blocking collectives: 30.1 us -> 0 us
  matrix products: 16.4 us -> 20.7 us
  starting transfers between devices: 0.12 us -> 3.85 us
    psum x1 -> x0, blocking collectives: 30.1 us -> none  [local(): dconv = lax.psum(partial_conv, 'ctx')]
    ppermute x0 -> x4, starting transfers between devices: none -> 3.73 us  [local(): lax.ppermute(dconv, 'ctx', [(i, i ^ far) for i in range(devices)])]
    unnamed x52 -> x46, local copies, waits for them, and re-layouts: 17.3 us -> 17.6 us
  transfers between devices with their start and end apart: 3 -> 7, of which waited for: 3 -> 3; matrix products, arithmetic and copies ran while one was open for 5% -> 13% of each run, Pallas kernels for 0% -> 0%
where the time goes in v1:
time: 218 us; the launch traced here: 217 us
  waiting for transfers between devices  137 us (63%)
  local copies, waits for them, and re-layouts  32.1 us (15%)
  matrix products  20.7 us (9%)
  between operations  14.1 us (6%)
  other arithmetic  9.73 us (4%)
  starting transfers between devices  3.85 us (2%)
    unnamed x4, waiting for transfers between devices  67 us
    all_gather x1, waiting for transfers between devices, local(): lax.all_gather(mem_keys, 'ctx', axis=0, tiled=True)  35.5 us
    all_gather x1, waiting for transfers between devices, local(): lax.all_gather(mem_vals, 'ctx', axis=0, tiled=True)  34.2 us
    unnamed x46, local copies, waits for them, and re-layouts  17.6 us
    concatenate x1, other arithmetic, local(): jnp.concatenate((dk_part.reshape(total_mem, width), dv_part.reshape(total...  4.46 us
  transfers between devices with their start and end apart: 7, of which 3 were waited for; matrix products, arithmetic and copies ran while one was open for 13% of the time, Pallas kernels for 0%

profile of v1, /device:TPU:0, one launch (start us, length us, event | category | flops | bytes accessed | tf_op | source)
XLA Modules:
  0.0 217.2 jit_solution(4071601867993659151)
XLA Ops:
  8.1 1.4 fusion.38
  10.2 1.3 fusion.36
  13.1 1.2 copy.80
  15.8 35.5 %all-gather.3.cloned.1.call-done = bf16[256,2048]{1,0:T(8,128)(2,1)} async-done(((bf16[16,2048]{1,0:T(8,128)(2,1)}), bf16[256,2048]{1,0:T(8,128)(2,1)}) %all-gather.3.cloned.1.call-update) | async-done | bytes 1048592 | tf_op jit(solution)/shard_map/all_gather | solution.py:47
  51.4 2.3 %copy.58 = bf16[256,2048]{0,1:T(8,128)(2,1)} copy(bf16[256,2048]{1,0:T(8,128)(2,1)} %all-gather.3.cloned.1.call-done) | data formatting | bytes 2097152 | tf_op jit(solution)/shard_map/all_gather | solution.py:47
  53.7 1.8 bitcast_reduce_fusion
  56.1 34.2 %all-gather.5.cloned.1.call-done = bf16[256,2048]{1,0:T(8,128)(2,1)} async-done(((bf16[16,2048]{1,0:T(8,128)(2,1)}), bf16[256,2048]{1,0:T(8,128)(2,1)}) %all-gather.5.cloned.1.call-update) | async-done | bytes 1048592 | tf_op jit(solution)/shard_map/all_gather | solution.py:48
  90.4 2.3 %copy.63 = bf16[256,2048]{0,1:T(8,128)(2,1)} copy(bf16[256,2048]{1,0:T(8,128)(2,1)} %all-gather.5.cloned.1.call-done) | data formatting | bytes 2097152 | tf_op jit(solution)/shard_map/all_gather | solution.py:48
  92.7 2.2 %fusion.3 = f32[16,128,128]{2,1,0:T(8,128)S(1)} fusion(bf16[256,16,128]{0,2,1:T(8,128)(2,1)} %bitcast.151, f32[16,256,128]{2,1,0:T(8,128)S(1)} %get-tuple-element.26, f32[16,128]{1,0:T(8,128)S(1)} %max.16, pred[256]{0:T(512)(128)(4,1)S(1)} %fusion.48), kind=kOutput, calls=%fused_computation.9 | convolution fusion | flops 136314880 | bytes 4202752 | tf_op jit(solution)/shard_map/hsn,nhd->hsd/dot_general | solution.py:61
  96.5 3.1 %fusion.19 = f32[16,256,128]{1,2,0:T(8,128)} fusion(bf16[128,16,128]{0,2,1:T(8,128)(2,1)} %copy.80, f32[16,256,128]{2,1,0:T(8,128)S(1)} %get-tuple-element.26, f32[16,128]{1,0:T(8,128)S(1)} %get-tuple-element.16, pred[256]{0:T(512)(128)(4,1)S(1)} %fusion.48), kind=kOutput, calls=%fused_computation.31 | convolution fusion | flops 136314880 | bytes 4727040 | tf_op jit(solution)/shard_map/hsn,shd->nhd/dot_general | solution.py:78
  101.9 1.8 copy.79
  103.7 4.5 %pad_maximum_fusion = f32[256,4096]{0,1:T(8,128)} fusion(f32[256,2048]{0,1:T(8,128)} %bitcast.140, f32[256,2048]{0,1:T(8,128)} %bitcast.141), kind=kLoop, calls=%fused_computation | loop fusion | flops 1048576 | bytes 8388608 | tf_op jit(solution)/shard_map/concatenate | solution.py:80
  108.2 5.6 %copy.125 = f32[256,4096]{1,0:T(8,128)} copy(f32[256,4096]{0,1:T(8,128)} %pad_maximum_fusion) | data formatting | bytes 8388608
  113.8 1.2 copy-done.2
  115.0 2.4 %fusion.17 = bf16[16,128,128]{1,2,0:T(8,128)(2,1)} fusion(bf16[128,16,128]{0,2,1:T(8,128)(2,1)S(1)} %copy-done.6, f32[16,128,128]{1,2,0:T(8,128)S(1)} %copy-done.2, f32[16,128]{1,0:T(8,128)S(1)} %copy.105, f32[16,128]{1,0:T(8,128)S(1)} %get-tuple-element.16, pred[128,128]{0,1:T(8,128)(4,1)S(1)} %iota_compare_fusion, bf16[128,2048]{1,0:T(8,128)(2,1)} %param.7), kind=kOutput, calls=%fused_computation.29 | convolution fusion | flops 68419584 | bytes 2654208 | tf_op jit(solution)/shard_map/shd,thd->hst/dot_general | solution.py:90
  117.4 1.4 convolution_bitcast_fusion.2
  118.8 66.9 %reduce-scatter.4.cloned.1.call-done = f32[16,4096]{1,0:T(8,128)} async-done(((f32[256,4096]{1,0:T(8,128)}), f32[16,4096]{1,0:T(8,128)}) %reduce-scatter.4.cloned.1.call-update) | async-done | bytes 262160
  187.4 1.2 multiply_reduce_fusion
  188.7 1.3 copy.127
  190.0 1.5 copy.129
  191.8 1.8 fusion.16
  193.7 1.0 copy.87
  195.0 1.5 copy.81
  197.1 1.6 broadcast_multiply_fusion
  198.8 1.6 copy.86
  200.4 2.1 collective-permute-start.2
  202.5 1.3 fusion.18
  203.8 1.6 copy.82
  205.4 1.1 collective-permute-start.3
  206.5 1.5 fusion.15
  208.1 1.0 copy.89
  209.1 1.0 copy.88
  (77 shorter events, 12.6 us)
Async XLA Ops:
  7.2 5.2 %copy-start.4 = (bf16[128,2048]{1,0:T(8,128)(2,1)S(1)}, bf16[128,2048]{1,0:T(8,128)(2,1)}, u32[]{:S(2)}) copy-start(bf16[128,2048]{1,0:T(8,128)(2,1)} %param.6) | copy-start | bytes 1572868
  7.2 5.5 %copy-start.14 = (bf16[128,2048]{1,0:T(8,128)(2,1)S(1)}, bf16[128,2048]{1,0:T(8,128)(2,1)}, u32[]{:S(2)}) copy-start(bf16[128,2048]{1,0:T(8,128)(2,1)} %param.5) | copy-start | bytes 1572868
  7.2 44.2 %all-gather.3.cloned.1.call-start = ((), (), s32[]{:S(2)}) async-start(), calls=%async_computation.1 | async-start | bytes 1114112 | tf_op jit(solution)/shard_map/all_gather | solution.py:47
  8.1 4.8 %copy-start.15 = (bf16[128,2048]{1,0:T(8,128)(2,1)S(1)}, bf16[128,2048]{1,0:T(8,128)(2,1)}, u32[]{:S(2)}) copy-start(bf16[128,2048]{1,0:T(8,128)(2,1)} %param.8) | copy-start | bytes 1572868
  10.2 80.2 %all-gather.5.cloned.1.call-start = ((), (), s32[]{:S(2)}) async-start(), calls=%async_computation.2 | async-start | bytes 1114112 | tf_op jit(solution)/shard_map/all_gather | solution.py:48
  12.3 173.5 %reduce-scatter.4.cloned.1.call-start = ((), (), s32[]{:S(2)}) async-start(), calls=%async_computation.3 | async-start | bytes 4456448
  12.6 2.1 copy-start.8
  14.7 1.0 copy-start
  92.7 2.2 %copy-start.1 = (f32[16,128,128]{1,2,0:T(8,128)S(1)}, f32[16,128,128]{1,2,0:T(8,128)}, u32[]{:S(2)}) copy-start(f32[16,128,128]{1,2,0:T(8,128)} %copy-done) | copy-start | bytes 3145732
  92.7 2.2 %copy-start.11 = (bf16[128,2048]{1,0:T(8,128)(2,1)S(1)}, bf16[128,2048]{1,0:T(8,128)(2,1)}, u32[]{:S(2)}) copy-start(bf16[128,2048]{1,0:T(8,128)(2,1)} %param.7) | copy-start | bytes 1572868
  96.5 3.1 %copy-start.6 = (bf16[128,16,128]{0,2,1:T(8,128)(2,1)S(1)}, bf16[128,16,128]{0,2,1:T(8,128)(2,1)}, u32[]{:S(2)}) copy-start(bf16[128,16,128]{0,2,1:T(8,128)(2,1)} %copy.80) | copy-start | bytes 1572868
  96.5 3.1 %copy-start.13 = (bf16[256,2048]{0,1:T(8,128)(2,1)S(1)}, bf16[256,2048]{0,1:T(8,128)(2,1)}, u32[]{:S(2)}) copy-start(bf16[256,2048]{0,1:T(8,128)(2,1)} %copy.63) | copy-start | bytes 3145732
  100.4 1.0 copy-start.9
  113.8 1.2 copy-start.2
  115.0 2.4 %copy-start.3 = (bf16[256,2048]{0,1:T(8,128)(2,1)S(1)}, bf16[256,2048]{0,1:T(8,128)(2,1)}, u32[]{:S(2)}) copy-start(bf16[256,2048]{0,1:T(8,128)(2,1)} %copy.58) | copy-start | bytes 3145732
  115.0 2.4 %copy-start.10 = (bf16[16,256,128]{2,1,0:T(8,128)(2,1)S(1)}, bf16[16,256,128]{2,1,0:T(8,128)(2,1)}, u32[]{:S(2)}) copy-start(bf16[16,256,128]{2,1,0:T(8,128)(2,1)} %copy-done.9) | copy-start | bytes 3145732
  187.1 4.5 %copy-start.5 = (bf16[128,2048]{1,0:T(8,128)(2,1)S(1)}, bf16[128,2048]{1,0:T(8,128)(2,1)}, u32[]{:S(2)}) copy-start(bf16[128,2048]{1,0:T(8,128)(2,1)} %param.6) | copy-start | bytes 1572868
  191.8 4.7 %collective-permute-start = (f32[8,16]{1,0:T(8,128)S(1)}, f32[8,16]{1,0:T(8,128)S(1)}, u32[]{:S(2)}, u32[]{:S(2)}) collective-permute-start(f32[8,16]{1,0:T(8,128)S(1)} %add_bitcast_fusion), channel_id=1, source_target_pairs={{0,1},{1,0},{2,3},{3,2},{4,5},{5,4},{6,7},{7,6},{8,9},{9,8},{10,11... | collective-permute-start | bytes 1544 | tf_op jit(solution)/shard_map/ppermute | solution.py:112
  193.7 3.4 %copy-start.16 = (f32[8,16]{1,0:T(8,128)S(1)}, f32[8,16]{1,0:T(8,128)}, u32[]{:S(2)}) copy-start(f32[8,16]{1,0:T(8,128)} %param.9) | copy-start | bytes 1540
  196.6 3.8 %collective-permute-start.1 = (f32[8,16]{1,0:T(8,128)S(1)}, f32[8,16]{1,0:T(8,128)S(1)}, u32[]{:S(2)}, u32[]{:S(2)}) collective-permute-start(f32[8,16]{1,0:T(8,128)S(1)} %add.62), channel_id=1, source_target_pairs={{0,2},{1,3},{2,0},{3,1},{4,6},{5,7},{6,4},{7,5},{8,10},{9,11},{10,... | collective-permute-start | bytes 1544 | tf_op jit(solution)/shard_map/ppermute | solution.py:112
  197.1 5.3 %copy-start.7 = (bf16[128,16,128]{0,2,1:T(8,128)(2,1)S(1)}, bf16[128,16,128]{0,2,1:T(8,128)(2,1)}, u32[]{:S(2)}) copy-start(bf16[128,16,128]{0,2,1:T(8,128)(2,1)} %copy.80) | copy-start | bytes 1572868
  200.4 5.0 %collective-permute-start.2 = (f32[8,16]{1,0:T(8,128)S(1)}, f32[8,16]{1,0:T(8,128)S(1)}, u32[]{:S(2)}, u32[]{:S(2)}) collective-permute-start(f32[8,16]{1,0:T(8,128)S(1)} %add.63), channel_id=1, source_target_pairs={{0,4},{1,5},{2,6},{3,7},{4,0},{5,1},{6,2},{7,3},{8,12},{9,13},{10,... | collective-permute-start | bytes 1544 | tf_op jit(solution)/shard_map/ppermute | solution.py:112
  203.7 4.3 %copy-start.12 = (bf16[128,16,128]{0,2,1:T(8,128)(2,1)S(1)}, bf16[128,16,128]{0,2,1:T(8,128)(2,1)}, u32[]{:S(2)}) copy-start(bf16[128,16,128]{0,2,1:T(8,128)(2,1)} %fusion.18) | copy-start | bytes 1572868
  205.4 4.7 %collective-permute-start.3 = (f32[8,16]{1,0:T(8,128)S(1)}, f32[8,16]{1,0:T(8,128)S(1)}, u32[]{:S(2)}, u32[]{:S(2)}) collective-permute-start(f32[8,16]{1,0:T(8,128)S(1)} %add.64), channel_id=1, source_target_pairs={{0,8},{1,9},{2,10},{3,11},{4,12},{5,13},{6,14},{7,15},{8,0},{9,1},... | collective-permute-start | bytes 1544 | tf_op jit(solution)/shard_map/ppermute | solution.py:112
Sparse Core Ops, SparseCore 0:
  10.7 40.5 all-gather.2
  53.5 36.8 all-gather.4
  114.0 71.7 reduce-scatter.3
